TPU v7x, 512 devices: a whole 4x8x8 slice. The times are simulated.
512 devices in a mesh: left: 16 (over x, y_hi, core), right: 32 (over y_lo, z).
Axes of the slice: x: 4, y: 8 (y_hi: 2, y_lo: 4; y = y_hi * 4 + y_lo), z: 8, core: 2. Of those that a mesh axis runs over, the one named last changes fastest.
Arguments:
- left_table: bfloat16 [32768, 256], P('left'), may hold values from -1.5 to 1.5
- right_table: bfloat16 [16, 16384, 256], P('left', 'right'), may hold values from -1.5 to 1.5
- relations: float32 [512, 256], replicated, may hold values from -6 to 6
- source_ids: int32 [16, 32, 1024], P('left', 'right'), may hold values from 0 to 2047
- relation_ids: int32 [16, 32, 1024], P('left', 'right'), may hold values from 0 to 511
- target_ids: int32 [16, 32, 1024], P('left', 'right'), may hold values from 0 to 511
- negative_ids: int32 [16, 32, 1, 1024], P('left', 'right'), may hold values from 0 to 511
- edge_counts: int32 [16, 32], P('left', 'right'), may hold values from 1 to 1024
Outputs:
- left_next: bfloat16 [32768, 256], P('left')
- right_next: bfloat16 [16, 16384, 256], P('left', 'right')
- relations_next: float32 [512, 256], replicated
Inputs may be any that keep to these rules, and one draw needn't show every extreme that they name: Edge slots at positions from edge_counts to 1023 hold ids but are padding.
All inputs are finite; a program needn't handle non-finite values.
Results may differ from a plain program's by a relative error of at most 0.0013.
Values may be sent and summed in bfloat16 or wider, within the bound.
No kernel may reach another device: no remote copies, remote signals or barrier semaphores. Data moves between devices by JAX's collectives and lax.ppermute only.
A program may use at most 64 MiB of HBM per device.

v0:
```python
import jax
import jax.numpy as jnp
from jax import lax
from jax.sharding import PartitionSpec as P

step_size = 0.5
relation_step = 12.0


def passed_along(array, axis, by):
    peers = lax.axis_size(axis)
    return lax.ppermute(array, axis, [(i, (i + by) % peers) for i in range(peers)])


def block_terms(left_blk, right_blk, relations, src, kind, dst, neg, live):
    half = relations.shape[1] // 2
    head = jnp.take(left_blk, src, axis=0).astype(jnp.float32)
    tail = jnp.take(right_blk, dst, axis=0).astype(jnp.float32)
    rel = jnp.take(relations, kind, axis=0)
    hre, him = (head[:, :half], head[:, half:])
    rre, rim = (rel[:, :half], rel[:, half:])
    query = jnp.concatenate([hre * rre - him * rim, hre * rim + him * rre], axis=1)
    q_low = query.astype(jnp.bfloat16)
    pos = jnp.sum(query * tail, axis=1)
    negrows = jnp.take(right_blk, neg, axis=0)
    scores = lax.dot_general(
        q_low, negrows, (((1,), (1,)), ((), ())), preferred_element_type=jnp.float32
    )
    c_pos = -jax.nn.sigmoid(-pos) * live
    c_neg = (jax.nn.sigmoid(scores) * (live[:, None] / neg.shape[0])).astype(jnp.bfloat16)
    g_query = jnp.dot(c_neg, negrows, preferred_element_type=jnp.float32) + c_pos[:, None] * tail
    g_neg = lax.dot_general(
        c_neg, q_low, (((0,), (0,)), ((), ())), preferred_element_type=jnp.float32
    )
    g_tail = c_pos[:, None] * query
    gre, gim = (g_query[:, :half], g_query[:, half:])
    grad_h = jnp.concatenate([gre * rre + gim * rim, -gre * rim + gim * rre], axis=1)
    grad_r = jnp.concatenate([gre * hre + gim * him, -gre * him + gim * hre], axis=1)
    return (grad_h, grad_r, g_tail, g_neg)


def shards(
    left_table,
    right_table,
    relations,
    source_ids,
    relation_ids,
    target_ids,
    negative_ids,
    edge_counts,
):
    right_blk = right_table[0]
    src_all = source_ids[0, 0]
    kind_all = relation_ids[0, 0]
    dst_all = target_ids[0, 0]
    negs = negative_ids[0, 0]
    count = edge_counts[0, 0]
    blocks = negs.shape[0]
    width = src_all.shape[0] // blocks
    live_blocks = (count + width - 1) // width

    def one(index, carry):
        lgrad, rgrad, tgrad = carry
        start = index * width
        n = lax.dynamic_index_in_dim(negs, index, 0, keepdims=False)
        live = (start + jnp.arange(width, dtype=jnp.int32) < count).astype(jnp.float32)
        grad_h, grad_r, g_tail, g_neg = block_terms(
            left_table, right_blk, relations, src_all, kind_all, dst_all, n, live
        )
        lgrad = lgrad.at[src_all].add(grad_h)
        rgrad = rgrad.at[kind_all].add(grad_r)
        tgrad = tgrad.at[dst_all].add(g_tail).at[n].add(g_neg)
        return (lgrad, rgrad, tgrad)

    init = (
        jnp.zeros(left_table.shape, jnp.float32),
        jnp.zeros(relations.shape, jnp.float32),
        jnp.zeros(right_blk.shape, jnp.float32),
    )
    left_grad, rel_grad, right_grad = lax.fori_loop(0, live_blocks, one, init)
    updated = (right_blk.astype(jnp.float32) - step_size * right_grad).astype(jnp.bfloat16)
    moved = passed_along(updated, "right", 1)
    left_total = lax.psum(left_grad, "right")
    rel_total = lax.psum(rel_grad, ("left", "right"))
    left_next = (left_table.astype(jnp.float32) - step_size * left_total).astype(jnp.bfloat16)
    relations_next = relations - relation_step * rel_total
    return (left_next, moved[None], relations_next)


def solution(mesh):
    return jax.shard_map(
        shards,
        mesh=mesh,
        in_specs=(
            P("left", None),
            P("left", "right", None),
            P(),
            P("left", "right", None),
            P("left", "right", None),
            P("left", "right", None),
            P("left", "right", None, None),
            P("left", "right"),
        ),
        out_specs=(P("left", None), P("left", "right", None), P()),
        check_vma=False,
    )
```

profile of v0, /device:TPU:2, one launch (start us, length us, event | category | flops | bytes accessed | tf_op | source)
XLA Modules:
  0.0 709.8 jit_solution(15141002125790694229)
XLA Ops:
  12.0 4.9 gather_fusion.4
  16.9 3.9 gather_fusion.6
  21.1 3.5 gather_fusion.5
  26.9 80.2 %while.17 = (s32[]{:T(128)}, f32[2048,256]{1,0:T(8,128)}, f32[512,256]{1,0:T(8,128)S(1)}, f32[512,256]{1,0:T(8,128)S(1)}, s32[]{:T(128)}, /*index=5*/s32[1024]{0...) while((s32[]{:T(128)}, f32[2048,256]{1,0:T(8,128)}, ...), condition=%wide.region_6.8_spmd, body=%wide.region_1.7_spmd.sunk | while | flops 1624953856 | bytes 75646288 | solution.py:80
  28.0 5.0 gather_fusion
  32.9 3.9 gather_fusion.3
  37.9 5.0 gather_fusion.2
  45.2 4.7 gather_fusion.1
  49.8 2.6 copy.26
  56.9 2.5 copy.31
  59.4 6.7 scatter_fusion.2
  66.2 3.0 multiply_convert_fusion.2
  72.8 6.7 scatter_fusion.3
  79.5 3.0 multiply_add_fusion.7
  83.6 2.5 copy.29
  86.1 9.4 %scatter_fusion = f32[2048,256]{1,0:T(8,128)} fusion(f32[2048,256]{1,0:T(8,128)} %get-tuple-element.393, s32[1024]{0:T(1024)S(1)} %bitcast.59, f32[1024,256]{1,0:T(8,128)} %copy.29), kind=kCustom, calls=%fused_computation.7.clone.1 | custom fusion | flops 262144 | bytes 3149824 | tf_op jit(solution)/shard_map/while/body/scatter-add | solution.py:70
  95.5 2.1 pad_maximum_fusion.6
  97.6 2.5 copy.30
  100.1 6.7 scatter_fusion.1
  108.8 4.3 collective-permute-start
  113.0 270.8 %all-reduce.5.cloned.1.call-done = f32[512,256]{1,0:T(8,128)} async-done(((f32[512,256]{1,0:T(8,128)}), f32[512,256]{1,0:T(8,128)}) %all-reduce.5.cloned.1.call-update) | async-done | bytes 524304 | tf_op jit(solution)/shard_map/psum | solution.py:84
  383.8 1.9 multiply_subtract_fusion.1
  385.7 313.7 %all-reduce.3.cloned.1.call-done = f32[2048,256]{1,0:T(8,128)} async-done(((f32[2048,256]{1,0:T(8,128)}), f32[2048,256]{1,0:T(8,128)}) %all-reduce.3.cloned.1.call-update) | async-done | bytes 2097168 | tf_op jit(solution)/shard_map/psum | solution.py:83
  699.4 2.8 subtract_convert_fusion
  (72 shorter events, 22.1 us)
Async XLA Ops:
  7.2 376.7 %all-reduce.5.cloned.1.call-start = ((), (), s32[]{:S(2)}) async-start(), calls=%async_computation.1 | async-start | bytes 1048576 | tf_op jit(solution)/shard_map/psum | solution.py:84
  12.0 4.9 copy-start
  16.9 4.2 copy-start.1
  24.9 2.0 copy-start.3
  24.9 2.0 copy-start.10
  24.9 2.0 copy-start.11
  25.0 2.0 copy-start.12
  25.0 2.0 copy-start.13
  52.4 1.5 copy-start.4
  54.0 1.0 copy-start.5
  55.0 0.8 copy-start.6
  66.2 3.0 copy-start.8
  66.2 3.0 copy-start.9
  69.2 1.8 copy-start.7
  107.1 0.8 copy-start.2
  107.9 591.5 %all-reduce.3.cloned.1.call-start = ((), (), s32[]{:S(2)}) async-start(), calls=%async_computation | async-start | bytes 4194304 | tf_op jit(solution)/shard_map/psum | solution.py:83
  108.8 277.0 %collective-permute-start = (bf16[512,256]{1,0:T(8,128)(2,1)S(1)}, bf16[512,256]{1,0:T(8,128)(2,1)S(1)}, u32[]{:S(2)}, u32[]{:S(2)}) collective-permute-start(bf16[512,256]{1,0:T(8,128)(2,1)S(1)} %subtract_convert_fusion.1), channel_id=1, source_target_pairs={{0,1},{1,2},{2,3},{3,4},{4,5},{5,6},{6,7},{7,8},{8,9},{9,10},{10,1... | collective-permute-start | bytes 786440 | tf_op jit(solution)/shard_map/ppermute | solution.py:12
Sparse Core Ops, SparseCore 0:
  108.1 275.7 all-reduce.4
  386.7 312.6 all-reduce.2
where the time goes:
time: 711 us; the launch traced here: 710 us
  waiting for transfers between devices  585 us (82%)
  other arithmetic  50.1 us (7%)
  local copies, waits for them, and re-layouts  48.1 us (7%)
  between operations  14.9 us (2%)
    psum x1, waiting for transfers between devices, shards(): left_total = lax.psum(left_grad, 'right')  314 us
    psum x1, waiting for transfers between devices, shards(): rel_total = lax.psum(rel_grad, ('left', 'right'))  271 us
  transfers between devices with their start and end apart: 3, of which 2 were waited for; matrix products, arithmetic and copies ran while one was open for 0% of the time, Pallas kernels for 0%

commit v1 on v0

--- a/solution.py
+++ b/solution.py
@@ -81,7 +81,7 @@
     updated = (right_blk.astype(jnp.float32) - step_size * right_grad).astype(jnp.bfloat16)
     moved = passed_along(updated, "right", 1)
     left_total = lax.psum(left_grad, "right")
-    rel_total = lax.psum(rel_grad, ("left", "right"))
+    rel_total = lax.psum(lax.psum(rel_grad, "left"), "right")
     left_next = (left_table.astype(jnp.float32) - step_size * left_total).astype(jnp.bfloat16)
     relations_next = relations - relation_step * rel_total
     return (left_next, moved[None], relations_next)

time: 711 us -> 630 us (0.89)
  waiting for transfers between devices: 585 us -> 507 us
    psum x1, waiting for transfers between devices: 271 us -> 180 us  [shards(): rel_total = lax.psum(lax.psum(rel_grad, 'left'), 'right')]
    ppermute x1, waiting for transfers between devices: 0.01 us -> 10.8 us  [passed_along(): lax.ppermute(array, axis, [(i, (i + by) % peers) for i in range(peers)])]
  transfers between devices with their start and end apart: 3 -> 3, of which waited for: 2 -> 3; matrix products, arithmetic and copies ran while one was open for 0% -> 0% of each run, Pallas kernels for 0% -> 0%
where the time goes in v1:
time: 630 us; the launch traced here: 629 us
  waiting for transfers between devices  507 us (80%)
  other arithmetic  49.1 us (8%)
  local copies, waits for them, and re-layouts  48 us (8%)
  between operations  14.9 us (2%)
  matrix products  6.52 us (1%)
    psum x1, waiting for transfers between devices, shards(): left_total = lax.psum(left_grad, 'right')  316 us
    psum x1, waiting for transfers between devices, shards(): rel_total = lax.psum(lax.psum(rel_grad, 'left'), 'right')  180 us
    scatter-add x2, other arithmetic, one(): tgrad = tgrad.at[dst_all].add(g_tail).at[n].add(g_neg)  13.5 us
  transfers between devices with their start and end apart: 3, of which 3 were waited for; matrix products, arithmetic and copies ran while one was open for 0% of the time, Pallas kernels for 0%

profile of v1, /device:TPU:2, one launch (start us, length us, event | category | flops | bytes accessed | tf_op | source)
XLA Modules:
  0.0 629.5 jit_solution(2600665460816306039)
XLA Ops:
  12.0 4.9 gather_fusion.4
  16.9 3.9 gather_fusion.6
  21.1 3.5 gather_fusion.5
  26.9 80.1 %while.17 = (s32[]{:T(128)}, f32[2048,256]{1,0:T(8,128)}, f32[512,256]{1,0:T(8,128)S(1)}, f32[512,256]{1,0:T(8,128)S(1)}, s32[]{:T(128)}, /*index=5*/s32[1024]{0...) while((s32[]{:T(128)}, f32[2048,256]{1,0:T(8,128)}, ...), condition=%wide.region_6.8_spmd, body=%wide.region_1.7_spmd.sunk | while | flops 1624953856 | bytes 75646288 | solution.py:80
  28.0 5.0 gather_fusion
  32.9 3.9 gather_fusion.3
  37.9 5.0 gather_fusion.2
  45.2 4.7 gather_fusion.1
  49.9 2.6 copy.26
  56.9 2.5 copy.31
  59.4 6.7 %scatter_fusion.2 = f32[512,256]{1,0:T(8,128)S(1)} fusion(f32[512,256]{1,0:T(8,128)S(1)} %get-tuple-element.397, s32[1024]{0:T(1024)S(1)} %bitcast.70, f32[1024,256]{1,0:T(8,128)} %copy.31), kind=kCustom, calls=%fused_computation.9.clone.1 | custom fusion | flops 262144 | bytes 3149824 | tf_op jit(solution)/shard_map/while/body/scatter-add | solution.py:72
  66.2 3.0 multiply_convert_fusion.2
  72.7 6.7 %scatter_fusion.3 = f32[512,256]{1,0:T(8,128)S(1)} fusion(f32[512,256]{1,0:T(8,128)S(1)} %scatter_fusion.2, s32[1024]{0:T(1024)S(1)} %bitcast.69, f32[1024,256]{1,0:T(8,128)} %fusion.31), kind=kCustom, calls=%fused_computation.10.clone.1 | custom fusion | flops 262144 | bytes 3149824 | tf_op jit(solution)/shard_map/while/body/scatter-add | solution.py:72
  79.5 3.0 multiply_add_fusion.7
  83.5 2.5 copy.29
  86.0 9.4 %scatter_fusion = f32[2048,256]{1,0:T(8,128)} fusion(f32[2048,256]{1,0:T(8,128)} %get-tuple-element.395, s32[1024]{0:T(1024)S(1)} %bitcast.59, f32[1024,256]{1,0:T(8,128)} %copy.29), kind=kCustom, calls=%fused_computation.7.clone.1 | custom fusion | flops 262144 | bytes 3149824 | tf_op jit(solution)/shard_map/while/body/scatter-add | solution.py:70
  95.4 2.1 pad_maximum_fusion.6
  97.5 2.5 copy.30
  100.1 6.7 %scatter_fusion.1 = f32[512,256]{1,0:T(8,128)S(1)} fusion(f32[512,256]{1,0:T(8,128)S(1)} %get-tuple-element.396, s32[1024]{0:T(1024)S(1)} %bitcast.57, f32[1024,256]{1,0:T(8,128)} %copy.30), kind=kCustom, calls=%fused_computation.8.clone.1 | custom fusion | flops 262144 | bytes 3149824 | tf_op jit(solution)/shard_map/while/body/scatter-add | solution.py:71
  107.9 180.2 %all-reduce.4.cloned.1.call-done = f32[512,256]{1,0:T(8,128)} async-done(((f32[512,256]{1,0:T(8,128)}), f32[512,256]{1,0:T(8,128)}) %all-reduce.4.cloned.1.call-update) | async-done | bytes 524304 | tf_op jit(solution)/shard_map/psum | solution.py:84
  288.2 3.1 collective-permute-start
  291.4 10.8 %collective-permute-done = bf16[512,256]{1,0:T(8,128)(2,1)S(1)} collective-permute-done((bf16[512,256]{1,0:T(8,128)(2,1)S(1)}, bf16[512,256]{1,0:T(8,128)(2,1)S(1)}, u32[]{:S(2)}, u32[]{:S(2)}) %collective-permute-start) | collective-permute-done | bytes 262176 | tf_op jit(solution)/shard_map/ppermute | solution.py:12
  302.1 316.0 %all-reduce.6.cloned.1.call-done = (f32[2048,256]{1,0:T(8,128)}, f32[512,256]{1,0:T(8,128)}) async-done(((f32[2048,256]{1,0:T(8,128)}, f32[512,256]{1,0:T(8,128)}), (f32[2048,256]{1,0:T(8,128)}, f32[512,256]{1,0:T(8,128)})) %all-reduce.6.cloned.1.call-update) | async-done | bytes 2621456 | tf_op jit(solution)/shard_map/psum | solution.py:83
  618.2 2.9 subtract_convert_fusion
  (74 shorter events, 22.3 us)
Async XLA Ops:
  7.2 281.0 %all-reduce.4.cloned.1.call-start = ((), (), s32[]{:S(2)}) async-start(), calls=%async_computation | async-start | bytes 1048576 | tf_op jit(solution)/shard_map/psum | solution.py:84
  12.0 4.9 copy-start
  16.9 4.2 copy-start.1
  24.9 2.0 copy-start.3
  24.9 2.0 copy-start.10
  24.9 2.0 copy-start.11
  25.0 2.0 copy-start.12
  25.0 2.0 copy-start.13
  52.4 1.5 copy-start.4
  54.0 1.0 copy-start.5
  55.0 0.8 copy-start.6
  66.1 3.0 copy-start.8
  66.2 3.0 copy-start.9
  69.2 1.8 copy-start.7
  107.0 0.8 copy-start.2
  107.9 510.3 %all-reduce.6.cloned.1.call-start = ((), (), s32[]{:S(2)}) async-start(), calls=%async_computation.1 | async-start | bytes 5242880 | tf_op jit(solution)/shard_map/psum | solution.py:83
  288.2 13.9 %collective-permute-start = (bf16[512,256]{1,0:T(8,128)(2,1)S(1)}, bf16[512,256]{1,0:T(8,128)(2,1)S(1)}, u32[]{:S(2)}, u32[]{:S(2)}) collective-permute-start(bf16[512,256]{1,0:T(8,128)(2,1)S(1)} %subtract_convert_fusion.1), channel_id=1, source_target_pairs={{0,1},{1,2},{2,3},{3,4},{4,5},{5,6},{6,7},{7,8},{8,9},{9,10},{10,1... | collective-permute-start | bytes 786440 | tf_op jit(solution)/shard_map/ppermute | solution.py:12
  618.2 2.9 copy-start.14
Sparse Core Ops, SparseCore 0:
  108.0 180.1 all-reduce.3
  291.1 326.9 all-reduce.5
